TPU v7x, 32 devices: a whole 2x2x4 slice. The times are simulated.
32 devices in a mesh: expert: 8 (over z, y), dp: 4 (over x, core).
Axes of the slice: x: 2, y: 2, z: 4, core: 2. Of those that a mesh axis runs over, the one named last changes fastest.
Arguments:
- tokens: bfloat16 [512, 7168], P('expert'), may hold values from -6 to 6
- expert_ids: int32 [512, 8], P('expert'), may hold values from 0 to 31, all different within a row; in each aligned block of 64 rows (0 to 63, 64 to 127, ...) at most 24 rows name the same one
- gate_weights: bfloat16 [512, 8], P('expert'), may hold values from 0.19921875 to 1
- w_gate: bfloat16 [32, 7168, 2048], P('expert', None, 'dp'), may hold values from -0.0625 to 0.0625
- w_up: bfloat16 [32, 7168, 2048], P('expert', None, 'dp'), may hold values from -0.0625 to 0.0625
- w_down: bfloat16 [32, 2048, 7168], P('expert', 'dp'), may hold values from -0.125 to 0.125
Outputs:
- layer_output: bfloat16 [512, 7168], P('expert')
Inputs may be any that keep to these rules, and one draw needn't show every extreme that they name: `expert_ids`: each token names 8 different experts. Among the 64 tokens of one index of expert (aligned blocks of rows), no expert is named more than 24 times, and in some blocks an expert is named exactly 24 times.
All inputs are finite; a program needn't handle non-finite values.
Results may differ from a plain program's by a relative error of at most 0.013.
Values may be sent and summed in bfloat16 or wider, within the bound.
No kernel may reach another device: no remote copies, remote signals or barrier semaphores. Data moves between devices by JAX's collectives and lax.ppermute only.
A program may use at most 192 MiB of HBM per device.

v0:
```python
import jax
import jax.numpy as jnp
from jax import lax
from jax.sharding import PartitionSpec as P

EXPERTS = 32
CAP = 24


def expert_block(pieces, w_gate, w_up, w_down):
    sources, per_device, slot_count, model_width = pieces.shape
    results = []
    for number in range(per_device):
        gathered = pieces[:, number].reshape(sources * slot_count, model_width)
        gate_proj = jnp.dot(gathered, w_gate[number], preferred_element_type=jnp.float32)
        up_proj = jnp.dot(gathered, w_up[number], preferred_element_type=jnp.float32)
        hidden = (jax.nn.silu(gate_proj) * up_proj).astype(jnp.bfloat16)
        result = jnp.dot(hidden, w_down[number], preferred_element_type=jnp.float32).astype(
            jnp.bfloat16
        )
        results.append(result.reshape(sources, slot_count, model_width))
    return jnp.stack(results, axis=1)


def place(expert_ids, capacity):
    matches = (
        expert_ids[:, :, None] == jnp.arange(EXPERTS, dtype=jnp.int32)[None, None, :]
    ).astype(jnp.int32)
    expert_hits = jnp.sum(matches, axis=1)
    earlier = jnp.cumsum(expert_hits, axis=0) - expert_hits
    position = jnp.sum(matches * earlier[:, None, :], axis=2)
    return expert_ids * capacity + position


def pack(tokens, slot_ids, total_slots):
    row_count, top_count = slot_ids.shape
    row_numbers = jnp.repeat(jnp.arange(row_count, dtype=jnp.int32), top_count)
    source_row = (
        jnp.full((total_slots,), row_count, jnp.int32).at[slot_ids.reshape(-1)].set(row_numbers)
    )
    padded_tokens = jnp.concatenate([tokens, jnp.zeros((1, tokens.shape[1]), tokens.dtype)], axis=0)
    return jnp.take(padded_tokens, source_row, axis=0)


def combine(returned, slot_ids, gate_weights):
    row_count, top_count = slot_ids.shape
    combined = jnp.zeros((row_count, returned.shape[1]), jnp.float32)
    for column in range(top_count):
        picked = jnp.take(returned, slot_ids[:, column], axis=0)
        combined = combined + gate_weights[:, column : column + 1].astype(jnp.float32) * picked
    return combined


def body(tokens, expert_ids, gate_weights, w_gate, w_up, w_down):
    model_width = tokens.shape[1]
    per_device = w_gate.shape[0]
    expert_count = lax.axis_size("expert")
    dp_size = lax.axis_size("dp")
    slot_ids = place(expert_ids, CAP)
    packed = pack(tokens, slot_ids, EXPERTS * CAP).reshape(
        expert_count, per_device, CAP, model_width
    )
    share = CAP // dp_size
    own_index = lax.axis_index("dp")
    mine = lax.dynamic_slice_in_dim(packed, own_index * share, share, 2)
    arrived = lax.all_to_all(mine, "expert", split_axis=0, concat_axis=0, tiled=True)
    outputs = expert_block(lax.all_gather(arrived, "dp", axis=2, tiled=True), w_gate, w_up, w_down)
    summed = lax.psum_scatter(
        outputs.astype(jnp.float32).astype(jnp.bfloat16), "dp", scatter_dimension=2, tiled=True
    ).astype(jnp.float32)
    returned = lax.all_to_all(
        summed.astype(jnp.bfloat16), "expert", split_axis=0, concat_axis=0, tiled=True
    ).astype(summed.dtype)
    returned = returned.reshape(EXPERTS * share, model_width)
    returned = jnp.concatenate([returned, jnp.zeros((1, model_width), jnp.float32)], axis=0)
    column_slot = slot_ids % CAP
    owner_expert = slot_ids // CAP
    in_share = column_slot // share == own_index
    local_ids = jnp.where(in_share, owner_expert * share + column_slot % share, EXPERTS * share)
    partial_value = combine(returned, local_ids, gate_weights)
    combined = lax.psum(partial_value.astype(jnp.bfloat16), "dp")
    return combined


def solution(mesh):
    placed = (
        P("expert", None),
        P("expert", None),
        P("expert", None),
        P("expert", None, "dp"),
        P("expert", None, "dp"),
        P("expert", "dp", None),
    )
    return jax.shard_map(
        body, mesh=mesh, in_specs=placed, out_specs=P("expert", None), check_vma=False
    )
```

profile of v0, /device:TPU:0, one launch (start us, length us, event | category | flops | bytes accessed | tf_op | source)
XLA Modules:
  0.0 544.2 jit_solution(12313884914584396794)
XLA Ops:
  6.5 0.7 convert_reduce_fusion
  7.3 0.1 copy.40
  7.3 0.1 reduce_window_sum.11
  7.4 0.1 copy.42
  7.5 0.7 select_reduce_fusion
  8.2 0.7 fusion.99
  9.0 0.1 copy.43
  9.0 0.1 reshape.65
  9.2 0.1 reshape.152
  9.2 2.4 scatter_custom_fusion
  11.7 0.1 broadcast_in_dim.41
  11.8 0.1 copy.44
  12.0 1.3 concatenate.8
  13.2 9.5 %gather_fusion = bf16[768,7168]{1,0:T(8,128)(2,1)} fusion(bf16[65,7168]{1,0:T(8,128)(2,1)S(1)} %concatenate.8, s32[1024]{0:T(1024)S(1)} %pad_clamp_fusion.8), kind=kCustom, calls=%fused_computation.8 | custom fusion | bytes 22023168 | tf_op jit(solution)/shard_map/jit(_take)/gather | solution.py:42
  22.7 4.2 constant_dynamic-slice_fusion
  27.0 3.7 copy_select_fusion
  30.7 69.7 %all_to_all.10 = bf16[8,4,6,7168]{3,1,2,0:T(4,128)(2,1)S(1)} all-to-all(bf16[8,4,6,7168]{3,1,2,0:T(4,128)(2,1)S(1)} %copy_select_fusion), channel_id=1, replica_groups=mesh['expert'=8,'dp'=4] {'expert'}, dimensions={0} | all-to-all | bytes 5505024 | tf_op jit(solution)/shard_map/all_to_all | solution.py:66
  100.5 3.2 copy.46
  103.6 0.0 all-gather.2.cloned.1.call-update
  103.6 0.0 reduce-scatter.2.cloned.1.call-start
  103.7 71.0 %all-gather.2.cloned.1.call-done = bf16[8,4,24,7168]{3,0,1,2:T(8,128)(2,1)} async-done(((bf16[8,4,6,7168]{3,0,1,2:T(8,128)(2,1)}), bf16[8,4,24,7168]{3,0,1,2:T(8,128)(2,1)}) %all-gather.2.cloned.1.call-update) | async-done | bytes 11010064 | tf_op jit(solution)/shard_map/all_gather | solution.py:67
  174.7 6.8 %fusion.108 = (bf16[8,1,24,7168]{3,0,1,2:T(8,128)(2,1)S(1)}, bf16[8,1,24,7168]{3,0,1,2:T(8,128)(2,1)}, bf16[8,1,24,7168]{3,0,1,2:T(8,128)(2,1)}, bf16[8,1,24,7168]{3,0,1,2:T(8,128)(2,1)S(1)}) fusion(bf16[8,4,24,7168]{3,0,1,2:T(8,128)(2,1)} %all-gather.2.cloned.1.call-done), kind=kLoop, calls=%fused_computation.159 | loop fusion | bytes 22020096 | tf_op jit(solution)/shard_map/slice | solution.py:14
  181.5 1.5 copy.57
  183.1 1.5 copy-done.5
  184.6 4.7 fusion.18
  189.2 10.7 %convolution_convert_fusion.3 = bf16[192,7168]{1,0:T(8,128)(2,1)} fusion(bf16[4,512,7168]{2,1,0:T(8,128)(2,1)} %param.13, bf16[192,7168]{1,0:T(8,128)(2,1)} %bitcast.128, bf16[4,7168,512]{2,1,0:T(8,128)(2,1)} %param.12, f32[192,512]{1,0:T(8,128)S(1)} %fusion.18), kind=kOutput, calls=%fused_computation.14 | convolution fusion | flops 2820538368 | bytes 20578304 | tf_op jit(solution)/shard_map/dot_general | solution.py:18
  199.9 5.0 copy.51
  204.9 1.5 copy.58
  206.4 1.6 copy-done.6
  208.0 4.7 fusion.13
  212.7 11.0 %convolution_convert_fusion.2 = bf16[192,7168]{1,0:T(8,128)(2,1)} fusion(bf16[4,512,7168]{2,1,0:T(8,128)(2,1)} %param.13, bf16[192,7168]{1,0:T(8,128)(2,1)} %bitcast.131, bf16[4,7168,512]{2,1,0:T(8,128)(2,1)} %param.12, f32[192,512]{1,0:T(8,128)S(1)} %fusion.13), kind=kOutput, calls=%fused_computation.13 | convolution fusion | flops 2820538368 | bytes 20578304 | tf_op jit(solution)/shard_map/dot_general | solution.py:18
  223.7 5.0 copy.52
  228.7 1.5 copy.59
  230.2 1.5 copy-done.7
  231.8 4.7 fusion.8
  236.4 10.7 %convolution_convert_fusion.1 = bf16[192,7168]{1,0:T(8,128)(2,1)} fusion(bf16[4,512,7168]{2,1,0:T(8,128)(2,1)} %param.13, bf16[192,7168]{1,0:T(8,128)(2,1)} %bitcast.134, bf16[4,7168,512]{2,1,0:T(8,128)(2,1)} %param.12, f32[192,512]{1,0:T(8,128)S(1)} %fusion.8), kind=kOutput, calls=%fused_computation.12 | convolution fusion | flops 2820538368 | bytes 20578304 | tf_op jit(solution)/shard_map/dot_general | solution.py:18
  247.2 4.8 copy.53
  252.0 1.5 copy.60
  253.5 1.6 copy-done.8
  255.1 4.7 fusion.3
  259.8 11.3 %convolution_convert_fusion = bf16[192,7168]{1,0:T(8,128)(2,1)} fusion(bf16[4,512,7168]{2,1,0:T(8,128)(2,1)} %param.13, bf16[192,7168]{1,0:T(8,128)(2,1)} %bitcast.137, bf16[4,7168,512]{2,1,0:T(8,128)(2,1)} %param.12, f32[192,512]{1,0:T(8,128)S(1)} %fusion.3), kind=kOutput, calls=%fused_computation.11 | convolution fusion | flops 2820538368 | bytes 20578304 | tf_op jit(solution)/shard_map/dot_general | solution.py:18
  271.1 3.4 copy.54
  274.6 5.1 pad_maximum_fusion
  279.7 0.0 reduce-scatter.2.cloned.1.call-update
  279.8 87.8 %reduce-scatter.2.cloned.1.call-done = bf16[8,4,6,7168]{3,0,1,2:T(8,128)(2,1)} async-done(((bf16[8,4,24,7168]{3,0,1,2:T(8,128)(2,1)}), bf16[8,4,6,7168]{3,0,1,2:T(8,128)(2,1)}) %reduce-scatter.2.cloned.1.call-update) | async-done | bytes 2752528 | tf_op jit(solution)/shard_map/reduce_scatter | solution.py:68
  367.6 5.4 copy.55
  373.0 5.6 %all-to-all-start.1 = ((bf16[8,4,6,7168]{3,1,2,0:T(4,128)(2,1)}), bf16[8,4,6,7168]{3,1,2,0:T(4,128)(2,1)S(1)}, u32[]{:S(2)}, u32[]{:S(2)}) async-start(bf16[8,4,6,7168]{3,1,2,0:T(4,128)(2,1)} %copy.55), calls=%async_computation.2 | async-start | bytes 5505024 | tf_op jit(solution)/shard_map/all_to_all | solution.py:71
  378.6 0.0 all-reduce.4.cloned.1.call-start
  378.8 62.0 %all-to-all-done.1 = bf16[8,4,6,7168]{3,1,2,0:T(4,128)(2,1)S(1)} async-done(((bf16[8,4,6,7168]{3,1,2,0:T(4,128)(2,1)}), bf16[8,4,6,7168]{3,1,2,0:T(4,128)(2,1)S(1)}, u32[]{:S(2)}, u32[]{:S(2)}) %all-to-all-start.1) | async-done | bytes 2752544 | tf_op jit(solution)/shard_map/all_to_all | solution.py:71
  440.8 2.7 copy.56
  443.5 3.4 reshape.67
  446.9 3.1 pad_convert_fusion
  450.0 4.6 gather_fusion.2
  454.6 5.7 %gather_fusion.3 = f32[64,7168]{1,0:T(8,128)} fusion(f32[193,7168]{1,0:T(8,128)} %pad_convert_fusion, s32[1024]{0:T(1024)S(1)} %get-tuple-element.55), kind=kCustom, calls=%fused_computation.2.clone | custom fusion | bytes 3670272 | tf_op jit(solution)/shard_map/jit(_take)/gather | solution.py:49
  460.3 5.7 %gather_fusion.4 = f32[64,7168]{1,0:T(8,128)} fusion(f32[193,7168]{1,0:T(8,128)} %pad_convert_fusion, s32[1024]{0:T(1024)S(1)} %get-tuple-element.54), kind=kCustom, calls=%fused_computation.3.clone | custom fusion | bytes 3670272 | tf_op jit(solution)/shard_map/jit(_take)/gather | solution.py:49
  466.0 5.8 %gather_fusion.5 = f32[64,7168]{1,0:T(8,128)} fusion(f32[193,7168]{1,0:T(8,128)} %pad_convert_fusion, s32[1024]{0:T(1024)S(1)} %get-tuple-element.53), kind=kCustom, calls=%fused_computation.4.clone | custom fusion | bytes 3670272 | tf_op jit(solution)/shard_map/jit(_take)/gather | solution.py:49
  471.8 5.7 %gather_fusion.6 = f32[64,7168]{1,0:T(8,128)} fusion(f32[193,7168]{1,0:T(8,128)} %pad_convert_fusion, s32[1024]{0:T(1024)S(1)} %get-tuple-element.52), kind=kCustom, calls=%fused_computation.5.clone | custom fusion | bytes 3670272 | tf_op jit(solution)/shard_map/jit(_take)/gather | solution.py:49
  477.5 5.8 %gather_fusion.7 = f32[64,7168]{1,0:T(8,128)} fusion(f32[193,7168]{1,0:T(8,128)} %pad_convert_fusion, s32[1024]{0:T(1024)S(1)} %get-tuple-element.51), kind=kCustom, calls=%fused_computation.6.clone | custom fusion | bytes 3670272 | tf_op jit(solution)/shard_map/jit(_take)/gather | solution.py:49
  483.4 5.8 %gather_fusion.1 = f32[64,7168]{1,0:T(8,128)} fusion(f32[193,7168]{1,0:T(8,128)} %pad_convert_fusion, s32[1024]{0:T(1024)S(1)} %get-tuple-element.57), kind=kCustom, calls=%fused_computation.clone | custom fusion | bytes 3670272 | tf_op jit(solution)/shard_map/jit(_take)/gather | solution.py:49
  489.1 5.7 %gather_fusion.8 = f32[64,7168]{1,0:T(8,128)} fusion(f32[193,7168]{1,0:T(8,128)} %pad_convert_fusion, s32[1024]{0:T(1024)S(1)} %get-tuple-element.50), kind=kCustom, calls=%fused_computation.7.clone | custom fusion | bytes 3670272 | tf_op jit(solution)/shard_map/jit(_take)/gather | solution.py:49
  494.8 6.5 %fusion.33 = bf16[64,7168]{1,0:T(8,128)(2,1)} fusion(f32[64,7168]{1,0:T(8,128)} %gather_fusion.8, f32[64,7168]{1,0:T(8,128)} %gather_fusion.7, f32[64,7168]{1,0:T(8,128)} %gather_fusion.6, f32[64,7168]{1,0:T(8,128)} %gather_fusion.5, f32[64,7168]{1,0:T(8,128)} %gather_fusion.4, f32[64,7168]{1,0:T(8,128)} %gather_fusion.3, f32[64,7168]{1,0:T(8,128)S(1)} %gather_fusion.2, ...), kind=kLoop, calls=%fused_computation.51 | loop fusion | flops 11010048 | bytes 15600128 | tf_op jit(solution)/shard_map/convert_element_type | solution.py:81
  501.4 0.0 all-reduce.4.cloned.1.call-update
  501.4 34.0 %all-reduce.4.cloned.1.call-done = bf16[64,7168]{1,0:T(8,128)(2,1)} async-done(((bf16[64,7168]{1,0:T(8,128)(2,1)}), bf16[64,7168]{1,0:T(8,128)(2,1)}) %all-reduce.4.cloned.1.call-update) | async-done | bytes 917520 | tf_op jit(solution)/shard_map/psum | solution.py:81
  535.4 2.2 copy.64
  (30 shorter events, 0.1 us)
Async XLA Ops:
  6.5 168.2 %all-gather.2.cloned.1.call-start = ((), (), s32[]{:S(2)}) async-start(), calls=%async_computation.3 | async-start | bytes 13762560 | tf_op jit(solution)/shard_map/all_gather | solution.py:67
  103.6 263.9 %reduce-scatter.2.cloned.1.call-start = ((), (), s32[]{:S(2)}) async-start(), calls=%async_computation.4 | async-start | bytes 13762560 | tf_op jit(solution)/shard_map/reduce_scatter | solution.py:68
  183.0 1.5 copy-start.5
  199.9 5.0 copy-start.3
  206.4 1.6 copy-start.6
  223.7 5.0 copy-start.1
  230.2 1.5 copy-start.7
  253.5 1.6 copy-start.8
  259.8 14.8 %copy-start.4 = (bf16[8,1,24,7168]{3,0,1,2:T(8,128)(2,1)S(1)}, bf16[8,1,24,7168]{3,0,1,2:T(8,128)(2,1)}, u32[]{:S(2)}) copy-start(bf16[8,1,24,7168]{3,0,1,2:T(8,128)(2,1)} %copy.53) | copy-start | bytes 8257540
  271.1 3.5 copy-start
  271.1 3.5 copy-start.2
  373.0 5.8 %copy-start.9 = (bf16[64,8]{0,1:T(8,128)(2,1)S(1)}, bf16[64,8]{0,1:T(8,128)(2,1)}, u32[]{:S(2)}) copy-start(bf16[64,8]{0,1:T(8,128)(2,1)} %param.10) | copy-start | bytes 3076
  373.0 67.8 %all-to-all-start.1 = ((bf16[8,4,6,7168]{3,1,2,0:T(4,128)(2,1)}), bf16[8,4,6,7168]{3,1,2,0:T(4,128)(2,1)S(1)}, u32[]{:S(2)}, u32[]{:S(2)}) async-start(bf16[8,4,6,7168]{3,1,2,0:T(4,128)(2,1)} %copy.55), calls=%async_computation.2 | async-start | bytes 5505024 | tf_op jit(solution)/shard_map/all_to_all | solution.py:71
  378.6 156.7 %all-reduce.4.cloned.1.call-start = ((), (), s32[]{:S(2)}) async-start(), calls=%async_computation.5 | async-start | bytes 1835008 | tf_op jit(solution)/shard_map/psum | solution.py:81
Sparse Core Ops, SparseCore 0:
  103.8 70.8 all-gather.1
  279.9 87.6 reduce-scatter.1
  501.5 33.8 all-reduce.3
where the time goes:
time: 553 us; the launch traced here: 544 us
  waiting for transfers between devices  255 us (46%)
  local copies, waits for them, and re-layouts  117 us (21%)
  blocking collectives  69.7 us (13%)
  matrix products  62.4 us (11%)
  other arithmetic  20.8 us (4%)
  between operations  13.6 us (2%)
  starting transfers between devices  5.73 us (1%)
    reduce_scatter x1, waiting for transfers between devices, body(): lax.psum_scatter(outputs.astype(jnp.float32).astype(jnp.bfloat16), 'dp',...  87.8 us
    all_gather x1, waiting for transfers between devices, body(): lax.all_gather(arrived, 'dp', axis=2, tiled=True)  71 us
    all_to_all x1, blocking collectives, body(): lax.all_to_all(mine, 'expert', split_axis=0, concat_axis=0, tiled=True)  69.7 us
    all_to_all x1, waiting for transfers between devices, body(): lax.all_to_all(summed.astype(jnp.bfloat16), 'expert', split_axis=0, conca...  62 us
    gather x8, local copies, waits for them, and re-layouts, combine(): picked = jnp.take(returned, slot_ids[:, column], axis=0)  44.9 us
    dot_general x4, matrix products, expert_block(): jnp.dot(hidden, w_down[number], preferred_element_type=jnp.float32)  43.7 us
    psum x1, waiting for transfers between devices, body(): combined = lax.psum(partial_value.astype(jnp.bfloat16), 'dp')  34 us
    dot_general x4, matrix products, expert_block(): jnp.dot(gathered, w_gate[number], preferred_element_type=jnp.float32)  18.6 us
  transfers between devices with their start and end apart: 4, of which 4 were waited for; matrix products, arithmetic and copies ran while one was open for 0% of the time, Pallas kernels for 0%

commit v1 on v0

v1 whole, which is shorter than its diff:
```python
import functools

import jax
import jax.numpy as jnp
from jax import lax
from jax.experimental import pallas as pl
from jax.experimental.pallas import tpu as pltpu
from jax.sharding import PartitionSpec as P

CAP = 24
META = 128

BF16 = jnp.bfloat16
F32 = jnp.float32


def dot(a, b):
    return jnp.dot(a, b, preferred_element_type=F32)


def up_kernel(
    experts,
    slots,
    top,
    place,
    meta_ref,
    own0,
    own1,
    far0,
    far1,
    gate_w,
    up_w,
    hidden_ref,
    mix_ref,
    pick,
    gate_acc,
    up_acc,
):
    column, number = pl.program_id(0), pl.program_id(1)
    rows = own0.shape[-2]

    @pl.when((column == 0) & (number == 0))
    def _():
        first = place[2] * experts
        lane = lax.broadcasted_iota(jnp.int32, (rows, META), 1)
        before = (
            lax.broadcasted_iota(jnp.int32, (rows, rows), 1)
            < lax.broadcasted_iota(jnp.int32, (rows, rows), 0)
        ).astype(BF16)
        wide = lax.broadcasted_iota(jnp.int32, (rows, experts * slots), 1)
        for half in range(2):
            ids = meta_ref[half, :, :top].astype(F32)
            weights = meta_ref[half, :, top : 2 * top].astype(F32)
            hits = jnp.zeros((rows, META), F32)
            value = []
            for e in range(experts):
                same = ids == (first + e).astype(F32)
                hit = jnp.sum(same.astype(F32), axis=1, keepdims=True)
                value.append(jnp.sum(jnp.where(same, weights, 0.0), axis=1, keepdims=True))
                hits = jnp.where(lane == e, hit, hits)
            rank = dot(before, hits.astype(BF16))
            target = jnp.full((rows, experts * slots), -1.0, F32)
            scale = jnp.zeros((rows, experts * slots), F32)
            for e in range(experts):
                mine = (wide >= e * slots) & (wide < (e + 1) * slots)
                at = jnp.where(hits[:, e : e + 1] > 0.0, rank[:, e : e + 1] + float(e * slots), -1.0)
                target = jnp.where(mine, at, target)
                scale = jnp.where(mine, value[e], scale)
            chosen = target == wide.astype(F32)
            mix_ref[half] = jnp.where(chosen, scale, 0.0).astype(BF16)
            pick[half] = jnp.transpose(chosen.astype(F32)).astype(BF16)

    def step(x0, x1):
        at = pl.ds(pl.multiple_of(number * slots, 8), slots)
        gathered = jnp.concatenate(
            [
                dot(pick[0, at, :], x0[...].reshape(x0.shape[-2:])).astype(BF16),
                dot(pick[1, at, :], x1[...].reshape(x1.shape[-2:])).astype(BF16),
            ],
            axis=0,
        )
        gate = dot(gathered, gate_w[...])
        up = dot(gathered, up_w[...])

        @pl.when(column == 0)
        def _():
            gate_acc[number] = gate
            up_acc[number] = up

        @pl.when(column > 0)
        def _():
            gate_acc[number] += gate
            up_acc[number] += up

    @pl.when(column < 2)
    def _():
        step(own0, own1)

    @pl.when(column >= 2)
    def _():
        step(far0, far1)

    @pl.when(column == pl.num_programs(0) - 1)
    def _():
        gate = gate_acc[number]
        hidden_ref[...] = (gate / (1.0 + jnp.exp(-gate)) * up_acc[number]).astype(BF16)


def quarter(column, place):
    far, side = column // 2, column % 2
    c = jnp.where(far == 1, 1 - place[0], place[0])
    x = jnp.where(side == 1, 1 - place[1], place[1])
    return x * 2 + c


def spot(role, side, half):
    return jnp.where(role == 0, side, half), jnp.where(role == 0, half, side)


def up_call(place, meta, own, far, gate_w, up_w, slots, top):
    experts, width, hidden = gate_w.shape
    rows, part = own.shape[-2:]

    def own_at(half):
        def at(column, number, place):
            a, b = spot(place[0], jnp.minimum(column, 1), half)
            return a, b, 0, 0

        return pl.BlockSpec((None, None, rows, part), at)

    def far_at(half):
        def at(column, number, place):
            a, b = spot(1 - place[0], jnp.maximum(column - 2, 0), half)
            return a, b, 0, 0

        return pl.BlockSpec((None, None, rows, part), at)

    weight = pl.BlockSpec(
        (None, part, hidden), lambda column, number, place: (number, quarter(column, place), 0)
    )
    return pl.pallas_call(
        functools.partial(up_kernel, experts, slots, top),
        grid_spec=pltpu.PrefetchScalarGridSpec(
            num_scalar_prefetch=1,
            grid=(width // part, experts),
            in_specs=[
                pl.BlockSpec((2, rows, META), lambda column, number, place: (0, 0, 0)),
                own_at(0),
                own_at(1),
                far_at(0),
                far_at(1),
                weight,
                weight,
            ],
            out_specs=[
                pl.BlockSpec(
                    (None, 2 * slots, hidden),
                    lambda column, number, place: (
                        jnp.where(column == width // part - 1, number, 0),
                        0,
                        0,
                    ),
                ),
                pl.BlockSpec(
                    (2, rows, experts * slots), lambda column, number, place: (0, 0, 0)
                ),
            ],
            scratch_shapes=[
                pltpu.VMEM((2, experts * slots, rows), BF16),
                pltpu.VMEM((experts, 2 * slots, hidden), F32),
                pltpu.VMEM((experts, 2 * slots, hidden), F32),
            ],
        ),
        out_shape=[
            jax.ShapeDtypeStruct((experts, 2 * slots, hidden), BF16),
            jax.ShapeDtypeStruct((2, rows, experts * slots), BF16),
        ],
        cost_estimate=pl.CostEstimate(
            flops=8 * experts * slots * width * hidden,
            bytes_accessed=4 * experts * width * hidden,
            transcendentals=0,
        ),
        name="up",
    )(place, meta, own, own, far, far, gate_w, up_w)


def down_kernel(
    experts, slots, place, hidden_ref, mix_ref, down_w, keep_ref, give_ref, result, ready, sems
):
    column, number = pl.program_id(0), pl.program_id(1)
    columns = pl.num_programs(0)
    slot = lax.rem(column, 2)
    value = dot(hidden_ref[number], down_w[...]).astype(BF16)
    at = pl.ds(pl.multiple_of(number * slots, 8), slots)
    result[0, at, :] = value[:slots]
    result[1, at, :] = value[slots:]

    def copy(column, half):
        slot = lax.rem(column, 2)
        side = lax.rem(column, 2)

        def give():
            a, b = spot(1 - place[0], side, half)
            return pltpu.make_async_copy(
                ready.at[slot, half], give_ref.at[a, b], sems.at[slot, half]
            )

        def keep():
            a, b = spot(place[0], side, half)
            return pltpu.make_async_copy(
                ready.at[slot, half], keep_ref.at[a, b], sems.at[slot, half]
            )

        return give, keep

    @pl.when(number == experts - 1)
    def _():
        for half in range(2):

            @pl.when(column >= 2)
            def _():
                copy(column - 2, half)[0]().wait()

            ready[slot, half] = dot(mix_ref[half], result[half]).astype(BF16)
            give, keep = copy(column, half)

            @pl.when(column < 2)
            def _():
                give().start()

            @pl.when(column >= 2)
            def _():
                keep().start()

        @pl.when(column == columns - 1)
        def _():
            for half in range(2):
                copy(column - 1, half)[1]().wait()
                copy(column, half)[1]().wait()


def down_call(place, hidden, mix, down_w, slots):
    experts, depth, width = down_w.shape
    rows = mix.shape[1]
    part = width // 4
    shape = jax.ShapeDtypeStruct((2, 2, rows, part), BF16)
    return pl.pallas_call(
        functools.partial(down_kernel, experts, slots),
        grid_spec=pltpu.PrefetchScalarGridSpec(
            num_scalar_prefetch=1,
            grid=(4, experts),
            in_specs=[
                pl.BlockSpec((experts, 2 * slots, depth), lambda column, number, place: (0, 0, 0)),
                pl.BlockSpec(
                    (2, rows, experts * slots), lambda column, number, place: (0, 0, 0)
                ),
                pl.BlockSpec(
                    (None, depth, part),
                    lambda column, number, place: (
                        number,
                        0,
                        quarter(jnp.where(column < 2, column + 2, column - 2), place),
                    ),
                ),
            ],
            out_specs=[pl.BlockSpec(memory_space=pl.ANY), pl.BlockSpec(memory_space=pl.ANY)],
            scratch_shapes=[
                pltpu.VMEM((2, experts * slots, part), BF16),
                pltpu.VMEM((2, 2, rows, part), BF16),
                pltpu.SemaphoreType.DMA((2, 2)),
            ],
        ),
        out_shape=[shape, shape],
        cost_estimate=pl.CostEstimate(
            flops=4 * experts * slots * width * depth,
            bytes_accessed=2 * experts * width * depth,
            transcendentals=0,
        ),
        name="down",
    )(place, hidden, mix, down_w)


def body(tokens, expert_ids, gate_weights, w_gate, w_up, w_down):
    count, width = tokens.shape
    groups, lanes = lax.axis_size("expert"), lax.axis_size("dp")
    top = expert_ids.shape[1]
    part = width // lanes
    ring = groups // 2
    slots = ring * CAP
    turn = list(range(0, ring, 2))[:1] + list(range(1, ring, 2)) + list(range(0, ring, 2))[:0:-1]

    def every(move):
        pairs = []
        for z in range(ring):
            for y in range(2):
                for x in range(2):
                    for c in range(2):
                        a, b, d, e = move(z, y, x, c)
                        pairs.append((((z * 2 + y) * 2 + x) * 2 + c, ((a * 2 + b) * 2 + d) * 2 + e))
        return pairs

    def send(value, move):
        return lax.ppermute(value, ("expert", "dp"), every(move))

    def along(step):
        def move(z, y, x, c):
            return turn[(turn.index(z) + step) % ring], y, x, c

        return move

    def first(z, y, x, c):
        return (z, y, 1 - x, c) if c == 0 else (z, 1 - y, x, c)

    def second(z, y, x, c):
        return (z, 1 - y, x, c) if c == 0 else (z, y, 1 - x, c)

    def other_x(z, y, x, c):
        return z, y, 1 - x, c

    def other_core(z, y, x, c):
        return z, y, x, 1 - c

    lane = lax.axis_index("dp")
    core, side, group = lane % 2, lane // 2, lax.axis_index("expert")
    place = jnp.stack([core, side, group]).astype(jnp.int32)

    meta = jnp.concatenate(
        [
            expert_ids.astype(BF16),
            gate_weights,
            jnp.zeros((count, META - 2 * top), BF16),
        ],
        axis=1,
    )
    piece = jnp.concatenate([lax.dynamic_slice_in_dim(tokens, lane * part, part, 1), meta], axis=1)
    arrived = [piece] + [send(piece, along(step)) for step in range(1, ring)]
    line = jnp.concatenate(arrived, axis=0)
    crossed = send(line, second)
    pair = jnp.stack([line, crossed])
    wide = jnp.concatenate([pair[None], send(pair, first)[None]], axis=0)
    far = send(wide, other_core)
    tags = jnp.stack(
        [
            line[:, part:],
            jnp.where(core == 0, wide[0, 1, :, part:], wide[1, 0, :, part:]),
        ]
    )
    own, far = wide[..., :part], far[..., :part]

    hidden, mix = up_call(place, tags, own, far, w_gate, w_up, slots, top)
    keep, give = down_call(place, hidden, mix, w_down, slots)

    total = keep.astype(F32) + send(give, other_core).astype(F32)
    total = total.astype(BF16)
    total = (total[0].astype(F32) + send(total[1], first).astype(F32)).astype(BF16)
    total = (total[0].astype(F32) + send(total[1], second).astype(F32)).astype(BF16)
    total = total.reshape(ring, count, part)
    result = total[0].astype(F32)
    for step in range(1, ring):
        result = result + send(total[step], along(ring - step)).astype(F32)
    result = result.astype(BF16)

    two = jnp.where(
        side == 0,
        jnp.stack([result, send(result, other_x)]),
        jnp.stack([send(result, other_x), result]),
    )
    back = send(two, other_core)
    four = jnp.where(core == 0, jnp.stack([two, back], axis=1), jnp.stack([back, two], axis=1))
    return jnp.transpose(four.reshape(lanes, count, part), (1, 0, 2)).reshape(count, width)


def solution(mesh):
    placed = (
        P("expert", None),
        P("expert", None),
        P("expert", None),
        P("expert", None, "dp"),
        P("expert", None, "dp"),
        P("expert", "dp", None),
    )
    return jax.shard_map(
        body, mesh=mesh, in_specs=placed, out_specs=P("expert", None), check_vma=False
    )
```

time: 553 us -> 220 us (0.40)
  the two profiles are of different devices: /device:TPU:0 before, /device:TPU:15 now
where the time goes in v1:
time: 220 us
  waiting for transfers between devices  125 us (57%)
  Pallas kernels  60.5 us (28%)
  starting transfers between devices  13.7 us (6%)
  other arithmetic  13 us (6%)
  local copies, waits for them, and re-layouts  7.24 us (3%)
    ppermute x14, waiting for transfers between devices, send(): return lax.ppermute(value, ('expert', 'dp'), every(move))  125 us
    pallas_call x1, Pallas kernels, up_call(): pl.pallas_call(functools.partial(up_kernel, experts, slots, top), grid_sp...  34.7 us
    pallas_call x1, Pallas kernels, down_call(): pl.pallas_call(functools.partial(down_kernel, experts, slots), grid_spec=...  25.9 us
    ppermute x14, starting transfers between devices, send(): return lax.ppermute(value, ('expert', 'dp'), every(move))  13.7 us
    concatenate x2, other arithmetic, body(): wide = jnp.concatenate([pair[None], send(pair, first)[None]], axis=0)  5.71 us
  transfers between devices with their start and end apart: 14, of which 14 were waited for; matrix products, arithmetic and copies ran while one was open for 3% of the time, Pallas kernels for 0%

profile of v1, /device:TPU:15, one launch (start us, length us, event | category | flops | bytes accessed | tf_op | source)
XLA Modules:
  0.0 219.8 jit_solution(10966462023914940805)
XLA Ops:
  0.0 0.0 copy-start
  0.0 0.8 convert_element_type.51
  0.8 0.1 copy.12
  0.9 0.8 copy.13
  1.7 0.0 copy-done
  1.7 0.1 concatenate.23
  1.8 0.2 collective-permute-start.2
  2.0 2.4 %collective-permute-start.1 = (bf16[64,1920]{1,0:T(8,128)(2,1)S(1)}, bf16[64,1920]{1,0:T(8,128)(2,1)S(1)}, u32[]{:S(2)}, u32[]{:S(2)}) collective-permute-start(bf16[64,1920]{1,0:T(8,128)(2,1)S(1)} %concatenate.23), channel_id=1, source_target_pairs={{0,24},{1,25},{2,26},{3,27},{4,28},{5,29},{6,30},{7,31},{8,16},{9,... | collective-permute-start | bytes 737288 | tf_op jit(solution)/shard_map/ppermute | solution.py:303
  4.5 2.0 collective-permute-start
  6.4 3.2 %collective-permute-done.2 = bf16[64,1920]{1,0:T(8,128)(2,1)S(1)} collective-permute-done((bf16[64,1920]{1,0:T(8,128)(2,1)S(1)}, bf16[64,1920]{1,0:T(8,128)(2,1)S(1)}, u32[]{:S(2)}, u32[]{:S(2)}) %collective-permute-start.2) | collective-permute-done | bytes 245792 | tf_op jit(solution)/shard_map/ppermute | solution.py:303
  9.6 11.5 %collective-permute-done.1 = bf16[64,1920]{1,0:T(8,128)(2,1)S(1)} collective-permute-done((bf16[64,1920]{1,0:T(8,128)(2,1)S(1)}, bf16[64,1920]{1,0:T(8,128)(2,1)S(1)}, u32[]{:S(2)}, u32[]{:S(2)}) %collective-permute-start.1) | collective-permute-done | bytes 245792 | tf_op jit(solution)/shard_map/ppermute | solution.py:303
  21.2 4.4 %collective-permute-done = bf16[64,1920]{1,0:T(8,128)(2,1)S(1)} collective-permute-done((bf16[64,1920]{1,0:T(8,128)(2,1)S(1)}, bf16[64,1920]{1,0:T(8,128)(2,1)S(1)}, u32[]{:S(2)}, u32[]{:S(2)}) %collective-permute-start) | collective-permute-done | bytes 245792 | tf_op jit(solution)/shard_map/ppermute | solution.py:303
  25.5 0.1 fusion.5
  25.7 0.0 copy-start.3
  25.7 0.3 collective-permute-start.3
  26.0 13.0 %collective-permute-done.3 = bf16[256,1920]{1,0:T(8,128)(2,1)S(1)} collective-permute-done((bf16[256,1920]{1,0:T(8,128)(2,1)S(1)}, bf16[256,1920]{1,0:T(8,128)(2,1)S(1)}, u32[]{:S(2)}, u32[]{:S(2)}) %collective-permute-start.3) | collective-permute-done | bytes 983072 | tf_op jit(solution)/shard_map/ppermute | solution.py:303
  39.0 0.0 copy-done.3
  39.0 0.3 fusion.4
  39.3 0.3 collective-permute-start.4
  39.6 23.5 %collective-permute-done.4 = bf16[2,256,1920]{2,1,0:T(8,128)(2,1)S(1)} collective-permute-done((bf16[2,256,1920]{2,1,0:T(8,128)(2,1)S(1)}, bf16[2,256,1920]{2,1,0:T(8,128)(2,1)S(1)}, u32[]{:S(2)}, u32[]{:S(2)}) %collective-permute-start.4) | collective-permute-done | bytes 1966112 | tf_op jit(solution)/shard_map/ppermute | solution.py:303
  63.1 0.0 copy-start.2
  63.1 2.5 %pad_maximum_fusion = bf16[2,2,256,1920]{3,2,1,0:T(8,128)(2,1)} fusion(bf16[1,2,256,1920]{3,2,1,0:T(8,128)(2,1)S(1)} %bitcast.37, bf16[1,2,256,1920]{3,2,1,0:T(8,128)(2,1)S(1)} %get-tuple-element.13), kind=kLoop, calls=%fused_computation.2 | loop fusion | flops 1966080 | bytes 7864320 | tf_op jit(solution)/shard_map/concatenate | solution.py:340
  65.6 0.0 copy-done.2
  65.6 2.2 %collective-permute-start.5 = (bf16[2,2,256,1920]{3,2,1,0:T(8,128)(2,1)}, bf16[2,2,256,1920]{3,2,1,0:T(8,128)(2,1)}, u32[]{:S(2)}, u32[]{:S(2)}) collective-permute-start(bf16[2,2,256,1920]{3,2,1,0:T(8,128)(2,1)} %pad_maximum_fusion), channel_id=1, source_target_pairs={{0,1},{1,0},{2,3},{3,2},{4,5},{5,4},{6,7},{7,6},{8,9},{9,8},{10,11... | collective-permute-start | bytes 11796488 | tf_op jit(solution)/shard_map/ppermute | solution.py:303
  67.8 0.7 pad_add_fusion.place
  68.4 0.8 slice_bitcast_fusion.4
  69.3 0.8 fusion.3
  70.1 0.7 pad_maximum_fusion.3.meta_ref
  70.8 3.2 %fusion.own0.own1 = bf16[2,2,256,1792]{3,2,1,0:T(8,128)(2,1)} fusion(bf16[1,2,256,1920]{3,2,1,0:T(8,128)(2,1)S(1)} %get-tuple-element.13, bf16[1,2,256,1920]{3,2,1,0:T(8,128)(2,1)} %bitcast.39), kind=kLoop, calls=%fused_computation.4 | loop fusion | flops 1835008 | bytes 7602176 | tf_op jit(solution)/shard_map/concatenate | solution.py:340
  74.0 0.5 collective-permute-done.5
  74.5 4.1 %slice.61.far0.far1 = bf16[2,2,256,1792]{3,2,1,0:T(8,128)(2,1)} slice(bf16[2,2,256,1920]{3,2,1,0:T(8,128)(2,1)} %collective-permute-done.5), slice={[0:2], [0:2], [0:256], [0:1792]} | slice | bytes 7340032 | tf_op jit(solution)/shard_map/slice | solution.py:348
  78.6 34.7 %up.1 = (bf16[4,192,512]{2,1,0:T(8,128)(2,1)}, bf16[2,256,384]{2,1,0:T(8,128)(2,1)}) custom-call(s32[3]{0:T(128)} %pad_add_fusion.place, bf16[2,256,128]{2,1,0:T(8,128)(2,1)} %pad_maximum_fusion.3.meta_ref, bf16[2,2,256,1792]{3,2,1,0:T(8,128)(2,1)} %fusion.own0.own1, bf16[2,2,256,1792]{3,2,1,0:T(8,128)(2,1)} %fusion.own0.own1, ...), custom_call_target="tpu_custom_call" | custom-call | flops 11274289152 | bytes 58720256 | tf_op jit(solution)/shard_map/up/pallas_call | solution.py:141
  113.3 25.9 %down.1 = (bf16[2,2,256,1792]{3,2,1,0:T(8,128)(2,1)}, bf16[2,2,256,1792]{3,2,1,0:T(8,128)(2,1)}) custom-call(s32[3]{0:T(128)} %pad_add_fusion.place, bf16[4,192,512]{2,1,0:T(8,128)(2,1)} %get-tuple-element.9.hidden_ref, bf16[2,256,384]{2,1,0:T(8,128)(2,1)} %get-tuple-element.10.mix_ref, bf16[4,512,7168]{2,1,0:T(8,128)(2,1)} %down_w.1), custom_call_target="tpu_custom_call" | custom-call | flops 5637144576 | bytes 29360128 | tf_op jit(solution)/shard_map/down/pallas_call | solution.py:247
  139.2 0.4 collective-permute-start.6
  139.6 6.2 %collective-permute-done.6 = bf16[2,2,256,1792]{3,2,1,0:T(8,128)(2,1)S(1)} collective-permute-done((bf16[2,2,256,1792]{3,2,1,0:T(8,128)(2,1)}, bf16[2,2,256,1792]{3,2,1,0:T(8,128)(2,1)S(1)}, u32[]{:S(2)}, u32[]{:S(2)}) %collective-permute-start.6) | collective-permute-done | bytes 3670048 | tf_op jit(solution)/shard_map/ppermute | solution.py:303
  145.9 2.9 %add_convert_fusion = bf16[2,2,256,1792]{3,2,1,0:T(8,128)(2,1)S(1)} fusion(bf16[2,2,256,1792]{3,2,1,0:T(8,128)(2,1)S(1)} %collective-permute-done.6, bf16[2,2,256,1792]{3,2,1,0:T(8,128)(2,1)} %get-tuple-element.11), kind=kLoop, calls=%fused_computation | loop fusion | flops 7340032 | bytes 11010048 | tf_op jit(solution)/shard_map/convert_element_type | solution.py:354
  148.8 0.1 slice_bitcast_fusion
  148.9 0.3 collective-permute-start.7
  149.2 22.1 %collective-permute-done.7 = bf16[2,256,1792]{2,1,0:T(8,128)(2,1)S(1)} collective-permute-done((bf16[2,256,1792]{2,1,0:T(8,128)(2,1)S(1)}, bf16[2,256,1792]{2,1,0:T(8,128)(2,1)S(1)}, u32[]{:S(2)}, u32[]{:S(2)}) %collective-permute-start.7) | collective-permute-done | bytes 1835040 | tf_op jit(solution)/shard_map/ppermute | solution.py:303
  171.3 0.5 fusion.1
  171.8 0.1 slice_bitcast_fusion.2
  171.9 0.3 collective-permute-start.8
  172.2 12.3 %collective-permute-done.8 = bf16[256,1792]{1,0:T(8,128)(2,1)S(1)} collective-permute-done((bf16[256,1792]{1,0:T(8,128)(2,1)S(1)}, bf16[256,1792]{1,0:T(8,128)(2,1)S(1)}, u32[]{:S(2)}, u32[]{:S(2)}) %collective-permute-start.8) | collective-permute-done | bytes 917536 | tf_op jit(solution)/shard_map/ppermute | solution.py:303
  184.5 0.2 fusion.2
  184.8 2.1 collective-permute-start.9
  186.9 1.1 collective-permute-start.11
  188.0 0.2 collective-permute-start.10
  188.2 3.7 %collective-permute-done.9 = bf16[64,1792]{1,0:T(8,128)(2,1)S(1)} collective-permute-done((bf16[64,1792]{1,0:T(8,128)(2,1)S(1)}, bf16[64,1792]{1,0:T(8,128)(2,1)S(1)}, u32[]{:S(2)}, u32[]{:S(2)}) %collective-permute-start.9) | collective-permute-done | bytes 229408 | tf_op jit(solution)/shard_map/ppermute | solution.py:303
  191.9 5.7 %collective-permute-done.11 = bf16[64,1792]{1,0:T(8,128)(2,1)S(1)} collective-permute-done((bf16[64,1792]{1,0:T(8,128)(2,1)S(1)}, bf16[64,1792]{1,0:T(8,128)(2,1)S(1)}, u32[]{:S(2)}, u32[]{:S(2)}) %collective-permute-start.11) | collective-permute-done | bytes 229408 | tf_op jit(solution)/shard_map/ppermute | solution.py:303
  197.6 11.2 %collective-permute-done.10 = bf16[64,1792]{1,0:T(8,128)(2,1)S(1)} collective-permute-done((bf16[64,1792]{1,0:T(8,128)(2,1)S(1)}, bf16[64,1792]{1,0:T(8,128)(2,1)S(1)}, u32[]{:S(2)}, u32[]{:S(2)}) %collective-permute-start.10) | collective-permute-done | bytes 229408 | tf_op jit(solution)/shard_map/ppermute | solution.py:303
  208.7 0.1 add_convert_fusion.1
  208.9 0.3 collective-permute-start.12
  209.2 6.4 %collective-permute-done.12 = bf16[64,1792]{1,0:T(8,128)(2,1)S(1)} collective-permute-done((bf16[64,1792]{1,0:T(8,128)(2,1)S(1)}, bf16[64,1792]{1,0:T(8,128)(2,1)S(1)}, u32[]{:S(2)}, u32[]{:S(2)}) %collective-permute-start.12) | collective-permute-done | bytes 229408 | tf_op jit(solution)/shard_map/ppermute | solution.py:303
  215.6 0.1 maximum_select_fusion.2
  215.7 1.4 collective-permute-start.13
  217.1 0.1 maximum_select_fusion.1
  217.1 1.4 collective-permute-done.13
  218.5 0.0 copy-start.1
  218.5 0.2 maximum_select_fusion
  218.7 0.1 copy.14
  218.8 1.0 copy.16
  219.8 0.0 copy-done.1
  (3 shorter events, 0.1 us)
Async XLA Ops:
  0.0 1.7 copy-start
  1.8 7.8 %collective-permute-start.2 = (bf16[64,1920]{1,0:T(8,128)(2,1)S(1)}, bf16[64,1920]{1,0:T(8,128)(2,1)S(1)}, u32[]{:S(2)}, u32[]{:S(2)}) collective-permute-start(bf16[64,1920]{1,0:T(8,128)(2,1)S(1)} %concatenate.23), channel_id=1, source_target_pairs={{0,16},{1,17},{2,18},{3,19},{4,20},{5,21},{6,22},{7,23},{8,0},{9,1... | collective-permute-start | bytes 737288 | tf_op jit(solution)/shard_map/ppermute | solution.py:303
  2.0 19.1 %collective-permute-start.1 = (bf16[64,1920]{1,0:T(8,128)(2,1)S(1)}, bf16[64,1920]{1,0:T(8,128)(2,1)S(1)}, u32[]{:S(2)}, u32[]{:S(2)}) collective-permute-start(bf16[64,1920]{1,0:T(8,128)(2,1)S(1)} %concatenate.23), channel_id=1, source_target_pairs={{0,24},{1,25},{2,26},{3,27},{4,28},{5,29},{6,30},{7,31},{8,16},{9,... | collective-permute-start | bytes 737288 | tf_op jit(solution)/shard_map/ppermute | solution.py:303
  4.5 21.1 %collective-permute-start = (bf16[64,1920]{1,0:T(8,128)(2,1)S(1)}, bf16[64,1920]{1,0:T(8,128)(2,1)S(1)}, u32[]{:S(2)}, u32[]{:S(2)}) collective-permute-start(bf16[64,1920]{1,0:T(8,128)(2,1)S(1)} %concatenate.23), channel_id=1, source_target_pairs={{0,8},{1,9},{2,10},{3,11},{4,12},{5,13},{6,14},{7,15},{8,24},{9,25... | collective-permute-start | bytes 737288 | tf_op jit(solution)/shard_map/ppermute | solution.py:303
  25.7 13.3 %copy-start.3 = (bf16[256,1920]{1,0:T(8,128)(2,1)}, bf16[256,1920]{1,0:T(8,128)(2,1)S(1)}, u32[]{:S(2)}) copy-start(bf16[256,1920]{1,0:T(8,128)(2,1)S(1)} %get-tuple-element.16) | copy-start | bytes 2949124
  25.7 13.3 %collective-permute-start.3 = (bf16[256,1920]{1,0:T(8,128)(2,1)S(1)}, bf16[256,1920]{1,0:T(8,128)(2,1)S(1)}, u32[]{:S(2)}, u32[]{:S(2)}) collective-permute-start(bf16[256,1920]{1,0:T(8,128)(2,1)S(1)} %get-tuple-element.16), channel_id=1, source_target_pairs={{0,4},{1,3},{2,6},{3,1},{4,0},{5,7},{6,2},{7,5},{8,12},{9,11},{10,... | collective-permute-start | bytes 2949128 | tf_op jit(solution)/shard_map/ppermute | solution.py:303
  39.3 23.8 %collective-permute-start.4 = (bf16[2,256,1920]{2,1,0:T(8,128)(2,1)S(1)}, bf16[2,256,1920]{2,1,0:T(8,128)(2,1)S(1)}, u32[]{:S(2)}, u32[]{:S(2)}) collective-permute-start(bf16[2,256,1920]{2,1,0:T(8,128)(2,1)S(1)} %get-tuple-element.14), channel_id=1, source_target_pairs={{0,2},{1,5},{2,0},{3,7},{4,6},{5,1},{6,4},{7,3},{8,10},{9,13},{10,... | collective-permute-start | bytes 5898248 | tf_op jit(solution)/shard_map/ppermute | solution.py:303
  63.1 2.5 %copy-start.2 = (bf16[2,256,1920]{2,1,0:T(8,128)(2,1)}, bf16[2,256,1920]{2,1,0:T(8,128)(2,1)S(1)}, u32[]{:S(2)}) copy-start(bf16[2,256,1920]{2,1,0:T(8,128)(2,1)S(1)} %collective-permute-done.4) | copy-start | bytes 5898244
  65.6 9.0 %collective-permute-start.5 = (bf16[2,2,256,1920]{3,2,1,0:T(8,128)(2,1)}, bf16[2,2,256,1920]{3,2,1,0:T(8,128)(2,1)}, u32[]{:S(2)}, u32[]{:S(2)}) collective-permute-start(bf16[2,2,256,1920]{3,2,1,0:T(8,128)(2,1)} %pad_maximum_fusion), channel_id=1, source_target_pairs={{0,1},{1,0},{2,3},{3,2},{4,5},{5,4},{6,7},{7,6},{8,9},{9,8},{10,11... | collective-permute-start | bytes 11796488 | tf_op jit(solution)/shard_map/ppermute | solution.py:303
  139.2 6.7 %collective-permute-start.6 = (bf16[2,2,256,1792]{3,2,1,0:T(8,128)(2,1)}, bf16[2,2,256,1792]{3,2,1,0:T(8,128)(2,1)S(1)}, u32[]{:S(2)}, u32[]{:S(2)}) collective-permute-start(bf16[2,2,256,1792]{3,2,1,0:T(8,128)(2,1)} %get-tuple-element.12), channel_id=1, source_target_pairs={{0,1},{1,0},{2,3},{3,2},{4,5},{5,4},{6,7},{7,6},{8,9},{9,8},{10,11... | collective-permute-start | bytes 11010056 | tf_op jit(solution)/shard_map/ppermute | solution.py:303
  148.9 22.4 %collective-permute-start.7 = (bf16[2,256,1792]{2,1,0:T(8,128)(2,1)S(1)}, bf16[2,256,1792]{2,1,0:T(8,128)(2,1)S(1)}, u32[]{:S(2)}, u32[]{:S(2)}) collective-permute-start(bf16[2,256,1792]{2,1,0:T(8,128)(2,1)S(1)} %slice_bitcast_fusion), channel_id=1, source_target_pairs={{0,2},{1,5},{2,0},{3,7},{4,6},{5,1},{6,4},{7,3},{8,10},{9,13},{10,... | collective-permute-start | bytes 5505032 | tf_op jit(solution)/shard_map/ppermute | solution.py:303
  171.9 12.6 %collective-permute-start.8 = (bf16[256,1792]{1,0:T(8,128)(2,1)S(1)}, bf16[256,1792]{1,0:T(8,128)(2,1)S(1)}, u32[]{:S(2)}, u32[]{:S(2)}) collective-permute-start(bf16[256,1792]{1,0:T(8,128)(2,1)S(1)} %slice_bitcast_fusion.2), channel_id=1, source_target_pairs={{0,4},{1,3},{2,6},{3,1},{4,0},{5,7},{6,2},{7,5},{8,12},{9,11},{10,... | collective-permute-start | bytes 2752520 | tf_op jit(solution)/shard_map/ppermute | solution.py:303
  184.8 7.1 %collective-permute-start.9 = (bf16[64,1792]{1,0:T(8,128)(2,1)S(1)}, bf16[64,1792]{1,0:T(8,128)(2,1)S(1)}, u32[]{:S(2)}, u32[]{:S(2)}) collective-permute-start(bf16[64,1792]{1,0:T(8,128)(2,1)S(1)} %get-tuple-element.17), channel_id=1, source_target_pairs={{0,16},{1,17},{2,18},{3,19},{4,20},{5,21},{6,22},{7,23},{8,0},{9,1... | collective-permute-start | bytes 688136 | tf_op jit(solution)/shard_map/ppermute | solution.py:303
  186.9 10.7 %collective-permute-start.11 = (bf16[64,1792]{1,0:T(8,128)(2,1)S(1)}, bf16[64,1792]{1,0:T(8,128)(2,1)S(1)}, u32[]{:S(2)}, u32[]{:S(2)}) collective-permute-start(bf16[64,1792]{1,0:T(8,128)(2,1)S(1)} %get-tuple-element.18), channel_id=1, source_target_pairs={{0,8},{1,9},{2,10},{3,11},{4,12},{5,13},{6,14},{7,15},{8,24},{9,25... | collective-permute-start | bytes 688136 | tf_op jit(solution)/shard_map/ppermute | solution.py:303
  188.0 20.7 %collective-permute-start.10 = (bf16[64,1792]{1,0:T(8,128)(2,1)S(1)}, bf16[64,1792]{1,0:T(8,128)(2,1)S(1)}, u32[]{:S(2)}, u32[]{:S(2)}) collective-permute-start(bf16[64,1792]{1,0:T(8,128)(2,1)S(1)} %get-tuple-element.19), channel_id=1, source_target_pairs={{0,24},{1,25},{2,26},{3,27},{4,28},{5,29},{6,30},{7,31},{8,16},{9,... | collective-permute-start | bytes 688136 | tf_op jit(solution)/shard_map/ppermute | solution.py:303
  208.9 6.7 %collective-permute-start.12 = (bf16[64,1792]{1,0:T(8,128)(2,1)S(1)}, bf16[64,1792]{1,0:T(8,128)(2,1)S(1)}, u32[]{:S(2)}, u32[]{:S(2)}) collective-permute-start(bf16[64,1792]{1,0:T(8,128)(2,1)S(1)} %add_convert_fusion.1), channel_id=1, source_target_pairs={{0,2},{1,3},{2,0},{3,1},{4,6},{5,7},{6,4},{7,5},{8,10},{9,11},{10,... | collective-permute-start | bytes 688136 | tf_op jit(solution)/shard_map/ppermute | solution.py:303
  215.7 2.9 %collective-permute-start.13 = (bf16[2,64,1792]{2,1,0:T(8,128)(2,1)S(1)}, bf16[2,64,1792]{2,1,0:T(8,128)(2,1)S(1)}, u32[]{:S(2)}, u32[]{:S(2)}) collective-permute-start(bf16[2,64,1792]{2,1,0:T(8,128)(2,1)S(1)} %maximum_select_fusion.2), channel_id=1, source_target_pairs={{0,1},{1,0},{2,3},{3,2},{4,5},{5,4},{6,7},{7,6},{8,9},{9,8},{10,11... | collective-permute-start | bytes 1376264 | tf_op jit(solution)/shard_map/ppermute | solution.py:303
  218.5 1.2 copy-start.1
